TPU v7x, 512 devices: a whole 4x4x16 slice. The times are simulated.
512 devices in a mesh: au: 16 (over y, x), vert: 32 (over z, core).
Axes of the slice: x: 4, y: 4, z: 16, core: 2. Of those that a mesh axis runs over, the one named last changes fastest.
Arguments:
- visibilities: bfloat16 [12288, 2, 2048], P(('au', 'vert')), may hold values from -6 to 6
- baseline_offsets: float32 [12288, 2, 128], P(('au', 'vert')), may hold values from -8 to 8
- channel_scale: float32 [16], replicated, may hold values from 0.8 to 1.25
- screen_depth: float32 [12288], P(('au', 'vert')), may hold values from -300 to 300
- stations: int32 [12288, 2], P(('au', 'vert')), may hold values from 0 to 511
- corners: int32 [12288, 2], P(('au', 'vert')), may hold values from 0 to 8191, as said below
- beam_terms: bfloat16 [512, 2, 1024], P(('au', 'vert')), may hold values from -5 to 5
Outputs:
- gridded: float32 [8192, 2, 8192], P('au', None, 'vert')
- dirty_image: float32 [8192, 2, 8192], P(('au', 'vert'))
Inputs may be any that keep to these rules, and one draw needn't show every extreme that they name: Subgrid s belongs to block d = floor(s / 24); with d = r * 32 + c, corners[s, 0] lies in [r * 512, (r + 1) * 512) and the columns corners[s, 1] to corners[s, 1] + 31 lie inside one column tile of 256 columns. At most 2 subgrids of one block lie in one column tile; for every r one column tile holds exactly 2 subgrids of every block of that r.
All inputs are finite; a program needn't handle non-finite values.
Results may differ from a plain program's by a relative error of at most 0.039.
Values may be sent and summed in bfloat16 or wider, within the bound.
A program may use at most 64 MiB of HBM per device.

v0:
```python
import math
import jax
import jax.numpy as jnp
from jax import lax
from jax.sharding import PartitionSpec as P

G = 8192
SUB = 32
field_view = 0.1
highest = lax.Precision.HIGHEST


def passed_along(value, axis, steps):
    count = lax.axis_size(axis)
    pairs = [(source, (source + steps) % count) for source in range(count)]
    return lax.ppermute(value, axis, pairs)


def complex_einsum(formula, left_operand_pair, right_pair):
    left_re, left_im = left_operand_pair
    right_re, right_im = right_pair
    real_part = jnp.einsum(formula, left_re, right_re, precision=highest) - jnp.einsum(
        formula, left_im, right_im, precision=highest
    )
    imag_part = jnp.einsum(formula, left_re, right_im, precision=highest) + jnp.einsum(
        formula, left_im, right_re, precision=highest
    )
    return (real_part, imag_part)


def complex_product(left_operand_pair, right_pair):
    return (
        left_operand_pair[0] * right_pair[0] - left_operand_pair[1] * right_pair[1],
        left_operand_pair[0] * right_pair[1] + left_operand_pair[1] * right_pair[0],
    )


def unit_table(row_count, col_count, period):
    product = (
        jnp.arange(row_count, dtype=jnp.int32)[:, None]
        * jnp.arange(col_count, dtype=jnp.int32)[None, :]
        % period
    )
    angle = 2.0 * math.pi / period * product.astype(jnp.float32)
    return (jnp.cos(angle), jnp.sin(angle))


def subgrid_table():
    centred = jnp.arange(SUB, dtype=jnp.int32) - SUB // 2
    product = centred[:, None] * centred[None, :] % SUB
    angle = -2.0 * math.pi / SUB * product.astype(jnp.float32)
    return (jnp.cos(angle) / SUB, jnp.sin(angle) / SUB)


def grid_subgrids(vis_items, offset_items, depth_items, beam_first, beam_second, channel_scale):
    item_count = vis_items.shape[0]
    vis_count = vis_items.shape[2]
    pixel_pos = jnp.arange(SUB, dtype=jnp.float32) - SUB // 2
    shift_u = (offset_items[:, 0, :, None] * channel_scale[None, None, :]).reshape(
        item_count, vis_count
    )
    shift_v = (offset_items[:, 1, :, None] * channel_scale[None, None, :]).reshape(
        item_count, vis_count
    )
    angle_u = 2.0 * math.pi / SUB * pixel_pos[None, :, None] * shift_u[:, None, :]
    angle_v = 2.0 * math.pi / SUB * pixel_pos[None, :, None] * shift_v[:, None, :]
    vis_re = vis_items[:, 0, None, :].astype(jnp.float32)
    vis_im = vis_items[:, 1, None, :].astype(jnp.float32)
    cos_u = jnp.cos(angle_u)
    sin_u = jnp.sin(angle_u)
    weighted_re = (vis_re * cos_u - vis_im * sin_u).astype(jnp.bfloat16)
    weighted_im = (vis_re * sin_u + vis_im * cos_u).astype(jnp.bfloat16)
    phasor_re = jnp.cos(angle_v).astype(jnp.bfloat16)
    phasor_im = jnp.sin(angle_v).astype(jnp.bfloat16)
    stacked_left = jnp.concatenate([weighted_re, weighted_im], axis=2)
    stacked_right = jnp.concatenate(
        [
            jnp.concatenate([phasor_re, -phasor_im], axis=2),
            jnp.concatenate([phasor_im, phasor_re], axis=2),
        ],
        axis=1,
    )
    sky_both = jnp.einsum(
        "npk,nqk->npq", stacked_left, stacked_right, preferred_element_type=jnp.float32
    )
    sky_pair = (sky_both[:, :, :SUB], sky_both[:, :, SUB:])
    taper_line = 1.0 - ((2.0 * jnp.arange(SUB, dtype=jnp.float32) + 1.0 - SUB) / SUB) ** 2
    taper_grid = taper_line[:, None] * taper_line[None, :] / math.sqrt(vis_count)
    sky_angle = pixel_pos * field_view / SUB
    radius_sq = sky_angle[:, None] ** 2 + sky_angle[None, :] ** 2
    screen_angle = -math.pi * depth_items[:, None, None] * radius_sq[None, :, :]
    first_beam = beam_first.astype(jnp.float32).reshape(item_count, 2, SUB, SUB)
    second_beam = beam_second.astype(jnp.float32).reshape(item_count, 2, SUB, SUB)
    pair_term = complex_product(
        (first_beam[:, 0], first_beam[:, 1]), (second_beam[:, 0], -second_beam[:, 1])
    )
    mixed = complex_product(sky_pair, pair_term)
    screened = complex_product(mixed, (jnp.cos(screen_angle), jnp.sin(screen_angle)))
    corrected = (screened[0] * taper_grid, screened[1] * taper_grid)
    dft_pair = subgrid_table()
    partial_pair = complex_einsum("ip,npq->niq", dft_pair, corrected)
    uv_pair = complex_einsum("niq,jq->nij", partial_pair, dft_pair)
    return jnp.stack(uv_pair, axis=1).reshape(item_count, 2 * SUB * SUB)


def grid_in_blocks(vis_items, offset_items, depth_items, first_items, second_items, channel_scale):
    item_count = vis_items.shape[0]
    block_size = math.gcd(item_count, 4)
    block_count = item_count // block_size

    def regroup(source):
        return source.reshape((block_count, block_size) + source.shape[1:])

    def grid_block(pieces):
        return grid_subgrids(
            pieces[0], pieces[1], pieces[2], pieces[3], pieces[4], channel_scale
        ).astype(jnp.bfloat16)

    gridded_blocks = lax.map(
        grid_block,
        (
            regroup(vis_items),
            regroup(offset_items),
            regroup(depth_items),
            regroup(first_items),
            regroup(second_items),
        ),
    )
    return gridded_blocks.reshape(item_count, 2 * SUB * SUB)


def add_subgrids(uv_items, offset_items, tile_rows, tile_cols):
    item_count = uv_items.shape[0]
    pieces = uv_items.reshape(item_count, 2, SUB, SUB)
    span_index = jnp.arange(SUB, dtype=jnp.int32)
    column_index = jnp.arange(tile_cols, dtype=jnp.int32)
    column_onehot = (
        column_index[None, None, :] == offset_items[:, 1, None, None] + span_index[None, :, None]
    ).astype(jnp.bfloat16)
    placed = jnp.einsum("mcij,mjv->micv", pieces, column_onehot, preferred_element_type=jnp.float32)
    row_ids = (offset_items[:, 0, None] + span_index[None, :]).reshape(-1)
    return jax.ops.segment_sum(
        placed.reshape(item_count * SUB, 2 * tile_cols), row_ids, num_segments=tile_rows + SUB
    )


def on_device(
    visibilities, baseline_offsets, channel_scale, screen_depth, stations, corners, beam_terms
):
    au_count = lax.axis_size("au")
    vertical_count = lax.axis_size("vert")
    device_count = au_count * vertical_count
    tile_rows = G // au_count
    tile_cols = G // vertical_count
    own_count = visibilities.shape[0]
    capacity = max(2, (2 * own_count + vertical_count - 1) // vertical_count)
    slot_count = vertical_count * capacity
    beam_table = lax.all_gather(beam_terms, ("au", "vert"), axis=0, tiled=True)
    target = corners[:, 1] // tile_cols
    row_offset = corners[:, 0] - lax.axis_index("au") * tile_rows
    col_offset = corners[:, 1] - target * tile_cols
    offsets = jnp.stack([row_offset, col_offset], axis=1)
    chosen = (target[:, None] == jnp.arange(vertical_count, dtype=jnp.int32)[None, :]).astype(
        jnp.int32
    )
    order_index = jnp.arange(own_count, dtype=jnp.int32)
    earlier_mask = (order_index[None, :] < order_index[:, None]).astype(jnp.int32)
    earlier_count = jnp.dot(earlier_mask, chosen)
    slot_rank = jnp.sum(chosen * earlier_count, axis=1)
    slot_index = target * capacity + slot_rank
    placement = jnp.arange(slot_count, dtype=jnp.int32)[:, None] == slot_index[None, :]
    place_whole = placement.astype(jnp.int32)
    uv_items = grid_in_blocks(
        visibilities,
        baseline_offsets,
        screen_depth,
        jnp.take(beam_table, stations[:, 0], axis=0),
        jnp.take(beam_table, stations[:, 1], axis=0),
        channel_scale,
    )
    uv_send = (
        jnp.dot(placement.astype(jnp.bfloat16), uv_items, preferred_element_type=jnp.float32)
        .astype(jnp.bfloat16)
        .reshape(vertical_count, capacity, -1)
    )
    offset_send = jnp.dot(place_whole, offsets).reshape(vertical_count, capacity, 2)
    uv_slots, offset_slots = (
        lax.all_to_all(uv_send, "vert", split_axis=0, concat_axis=0, tiled=True),
        lax.all_to_all(offset_send, "vert", split_axis=0, concat_axis=0, tiled=True),
    )
    extended = add_subgrids(
        uv_slots.reshape(slot_count, 2 * SUB * SUB),
        offset_slots.reshape(slot_count, 2),
        tile_rows,
        tile_cols,
    )
    carried = passed_along(extended[tile_rows:].astype(jnp.bfloat16), "au", 1).astype(jnp.float32)
    uv_tile = extended[:tile_rows].at[:SUB].add(carried).reshape(tile_rows, 2, tile_cols)
    block_rows = G // device_count
    row_blocks = lax.all_to_all(
        uv_tile.astype(jnp.bfloat16), "vert", split_axis=0, concat_axis=2, tiled=True
    ).astype(uv_tile.dtype)
    split_rows = row_blocks.reshape(block_rows, 2, block_rows, device_count)
    short_table = unit_table(block_rows, block_rows, block_rows)
    long_table = unit_table(device_count, device_count, device_count)
    twist_cols = unit_table(block_rows, device_count, G)
    first_pass = complex_einsum("urj,kr->ukj", (split_rows[:, 0], split_rows[:, 1]), short_table)
    first_pass = complex_product(first_pass, (twist_cols[0][None], twist_cols[1][None]))
    second_pass = complex_einsum("ukj,pj->pku", first_pass, long_table)
    spectra = jnp.stack(second_pass, axis=1).reshape(
        au_count, vertical_count, 2, block_rows * block_rows
    )
    arrived = lax.all_to_all(
        lax.all_to_all(spectra.astype(jnp.bfloat16), "au", split_axis=0, concat_axis=0, tiled=True),
        "vert",
        split_axis=1,
        concat_axis=1,
        tiled=True,
    ).astype(spectra.dtype)
    whole_rows = arrived.reshape(device_count, 2, block_rows, block_rows)
    third_pass = complex_einsum("jkl,qj->qkl", (whole_rows[:, 0], whole_rows[:, 1]), long_table)
    twist_rows = unit_table(device_count, block_rows, G)
    third_pass = complex_product(third_pass, (twist_rows[0][:, None, :], twist_rows[1][:, None, :]))
    fourth_pass = complex_einsum("qkl,pl->kpq", third_pass, short_table)
    image_scale = 1.0 / (SUB * math.sqrt(own_count * device_count))
    dirty_image = jnp.stack(fourth_pass, axis=1).reshape(block_rows, 2, G) * image_scale
    return (uv_tile, dirty_image)


def solution(mesh):
    return jax.shard_map(
        on_device,
        mesh=mesh,
        in_specs=(
            P(("au", "vert"), None, None),
            P(("au", "vert"), None, None),
            P(),
            P(("au", "vert")),
            P(("au", "vert"), None),
            P(("au", "vert"), None),
            P(("au", "vert"), None, None),
        ),
        out_specs=(P("au", None, "vert"), P(("au", "vert"), None, None)),
        check_vma=False,
    )
```

profile of v0, /device:TPU:1, one launch (start us, length us, event | category | flops | bytes accessed | tf_op | source)
XLA Modules:
  0.0 559.0 jit_solution(18145819555831487277)
XLA Ops:
  7.9 0.8 multiply_subtract_fusion.6
  9.0 0.7 multiply_add_fusion.5
  10.6 16.7 %all-to-all-start = ((s32[32,2,2]{1,2,0:T(2,128)}), s32[32,2,2]{1,2,0:T(2,128)S(1)}, u32[]{:S(2)}, u32[]{:S(2)}) async-start(s32[32,2,2]{1,2,0:T(2,128)} %copy.49), calls=%async_computation | async-start | bytes 65536 | tf_op jit(solution)/shard_map/all_to_all | solution.py:189
  27.3 0.7 reshape.464
  28.1 0.8 compare_and_fusion
  28.9 185.3 %all-gather.2.cloned.1.call-done = bf16[512,2,1024]{2,1,0:T(2,128)(2,1)} async-done(((bf16[1,2,1024]{2,1,0:T(2,128)(2,1)}), bf16[512,2,1024]{2,1,0:T(2,128)(2,1)}) %all-gather.2.cloned.1.call-update) | async-done | bytes 2097168 | tf_op jit(solution)/shard_map/all_gather | solution.py:158
  214.1 2.3 gather_fusion
  216.5 2.3 gather_fusion.1
  219.1 119.9 %while.15 = (s32[]{:T(128)}, bf16[6,4,2048]{2,1,0:T(4,128)(2,1)S(1)}, bf16[6,4,2,2048]{3,2,1,0:T(2,128)(2,1)}, f32[6,4,2,128]{3,2,1,0:T(2,128)}, f32[16]{0:T(128...) while((s32[]{:T(128)}, ...), condition=%wide.region_2.4_spmd, body=%wide.region_1.3_spmd.sunk | while | flops 94977376 | bytes 7133457 | solution.py:119
  221.2 0.8 constant_dynamic-slice_fusion.8
  222.0 8.0 %fusion.347 = (bf16[4,32,2048]{2,1,0:T(8,128)(2,1)S(1)}, bf16[4,32,2048]{2,1,0:T(8,128)(2,1)S(1)}, bf16[4,32,2048]{2,1,0:T(8,128)(2,1)S(1)}, bf16[4,32,2048]{2,1,0:T(8,128)(2,1)S(1)}) fusion(f32[4,2048]{1,0:T(4,128)S(1)} %get-tuple-element.319, f32[4,2048]{1,0:T(4,128)S(1)} %get-tuple-element.322, f32[32]{0:T(128)S(1)} %fusion.346, ...), kind=kLoop, calls=%fused_computation.30.clone.1 | loop fusion | flops 3145728 | bytes 2228352 | tf_op jit(solution)/shard_map/while/body/eval_jaxpr/convert_element_type | solution.py:71
  230.0 3.6 fusion.348
  233.6 0.8 fusion.349
  241.1 0.8 constant_dynamic-slice_fusion.8
  242.0 8.0 %fusion.347 = (bf16[4,32,2048]{2,1,0:T(8,128)(2,1)S(1)}, bf16[4,32,2048]{2,1,0:T(8,128)(2,1)S(1)}, bf16[4,32,2048]{2,1,0:T(8,128)(2,1)S(1)}, bf16[4,32,2048]{2,1,0:T(8,128)(2,1)S(1)}) fusion(f32[4,2048]{1,0:T(4,128)S(1)} %get-tuple-element.319, f32[4,2048]{1,0:T(4,128)S(1)} %get-tuple-element.322, f32[32]{0:T(128)S(1)} %fusion.346, ...), kind=kLoop, calls=%fused_computation.30.clone.1 | loop fusion | flops 3145728 | bytes 2228352 | tf_op jit(solution)/shard_map/while/body/eval_jaxpr/convert_element_type | solution.py:71
  250.0 3.6 fusion.348
  253.6 0.8 fusion.349
  261.1 0.8 constant_dynamic-slice_fusion.8
  262.0 8.0 %fusion.347 = (bf16[4,32,2048]{2,1,0:T(8,128)(2,1)S(1)}, bf16[4,32,2048]{2,1,0:T(8,128)(2,1)S(1)}, bf16[4,32,2048]{2,1,0:T(8,128)(2,1)S(1)}, bf16[4,32,2048]{2,1,0:T(8,128)(2,1)S(1)}) fusion(f32[4,2048]{1,0:T(4,128)S(1)} %get-tuple-element.319, f32[4,2048]{1,0:T(4,128)S(1)} %get-tuple-element.322, f32[32]{0:T(128)S(1)} %fusion.346, ...), kind=kLoop, calls=%fused_computation.30.clone.1 | loop fusion | flops 3145728 | bytes 2228352 | tf_op jit(solution)/shard_map/while/body/eval_jaxpr/convert_element_type | solution.py:71
  270.0 3.6 fusion.348
  273.6 0.8 fusion.349
  281.1 0.8 constant_dynamic-slice_fusion.8
  282.0 8.0 %fusion.347 = (bf16[4,32,2048]{2,1,0:T(8,128)(2,1)S(1)}, bf16[4,32,2048]{2,1,0:T(8,128)(2,1)S(1)}, bf16[4,32,2048]{2,1,0:T(8,128)(2,1)S(1)}, bf16[4,32,2048]{2,1,0:T(8,128)(2,1)S(1)}) fusion(f32[4,2048]{1,0:T(4,128)S(1)} %get-tuple-element.319, f32[4,2048]{1,0:T(4,128)S(1)} %get-tuple-element.322, f32[32]{0:T(128)S(1)} %fusion.346, ...), kind=kLoop, calls=%fused_computation.30.clone.1 | loop fusion | flops 3145728 | bytes 2228352 | tf_op jit(solution)/shard_map/while/body/eval_jaxpr/convert_element_type | solution.py:71
  289.9 3.6 fusion.348
  293.5 0.8 fusion.349
  301.1 0.8 constant_dynamic-slice_fusion.8
  301.9 8.0 %fusion.347 = (bf16[4,32,2048]{2,1,0:T(8,128)(2,1)S(1)}, bf16[4,32,2048]{2,1,0:T(8,128)(2,1)S(1)}, bf16[4,32,2048]{2,1,0:T(8,128)(2,1)S(1)}, bf16[4,32,2048]{2,1,0:T(8,128)(2,1)S(1)}) fusion(f32[4,2048]{1,0:T(4,128)S(1)} %get-tuple-element.319, f32[4,2048]{1,0:T(4,128)S(1)} %get-tuple-element.322, f32[32]{0:T(128)S(1)} %fusion.346, ...), kind=kLoop, calls=%fused_computation.30.clone.1 | loop fusion | flops 3145728 | bytes 2228352 | tf_op jit(solution)/shard_map/while/body/eval_jaxpr/convert_element_type | solution.py:71
  309.9 3.6 fusion.348
  313.5 0.8 fusion.349
  321.1 0.8 constant_dynamic-slice_fusion.8
  321.9 8.0 %fusion.347 = (bf16[4,32,2048]{2,1,0:T(8,128)(2,1)S(1)}, bf16[4,32,2048]{2,1,0:T(8,128)(2,1)S(1)}, bf16[4,32,2048]{2,1,0:T(8,128)(2,1)S(1)}, bf16[4,32,2048]{2,1,0:T(8,128)(2,1)S(1)}) fusion(f32[4,2048]{1,0:T(4,128)S(1)} %get-tuple-element.319, f32[4,2048]{1,0:T(4,128)S(1)} %get-tuple-element.322, f32[32]{0:T(128)S(1)} %fusion.346, ...), kind=kLoop, calls=%fused_computation.30.clone.1 | loop fusion | flops 3145728 | bytes 2228352 | tf_op jit(solution)/shard_map/while/body/eval_jaxpr/convert_element_type | solution.py:71
  329.9 3.6 fusion.348
  333.5 0.8 fusion.349
  339.2 0.9 reshape.466
  340.1 7.4 %all-to-all-start.1 = ((bf16[32,2,2048]{2,1,0:T(2,128)(2,1)}), bf16[32,2,2048]{2,1,0:T(2,128)(2,1)S(1)}, u32[]{:S(2)}, u32[]{:S(2)}) async-start(bf16[32,2,2048]{2,1,0:T(2,128)(2,1)} %reshape.466), calls=%async_computation.1 | async-start | bytes 524288 | tf_op jit(solution)/shard_map/all_to_all | solution.py:188
  347.9 21.8 %all-to-all-done.1 = bf16[32,2,2048]{2,1,0:T(2,128)(2,1)S(1)} async-done(((bf16[32,2,2048]{2,1,0:T(2,128)(2,1)}), bf16[32,2,2048]{2,1,0:T(2,128)(2,1)S(1)}, u32[]{:S(2)}, u32[]{:S(2)}) %all-to-all-start.1) | async-done | bytes 262176 | tf_op jit(solution)/shard_map/all_to_all | solution.py:188
  370.2 1.0 convolution_bitcast_fusion
  371.2 3.9 copy.56
  375.1 2.4 copy.81
  377.5 13.5 %scatter_custom_fusion = f32[544,512]{1,0:T(8,128)S(1)} fusion(s32[2048]{0:T(1024)S(1)} %reshape.493, f32[2048,512]{1,0:T(8,128)} %bitcast.254, f32[]{:T(128)} %constant.250.clone.1), kind=kCustom, calls=%fused_computation.192 | custom fusion | flops 1048576 | bytes 1114624 | tf_op jit(solution)/shard_map/scatter-add | solution.py:142
  391.0 3.2 collective-permute-start
  394.2 1.0 slice.178
  395.2 3.7 collective-permute-done
  399.6 1.9 reshape.468
  401.5 1.2 convert_element_type.204
  402.7 5.8 %all-to-all-start.2 = ((bf16[512,2,256]{2,1,0:T(2,128)(2,1)}), bf16[512,2,256]{2,1,0:T(2,128)(2,1)S(1)}, u32[]{:S(2)}, u32[]{:S(2)}) async-start(bf16[512,2,256]{2,1,0:T(2,128)(2,1)} %convert_element_type.204), calls=%async_computation.2 | async-start | bytes 1048576 | tf_op jit(solution)/shard_map/all_to_all | solution.py:200
  408.6 33.0 %all-to-all-done.2 = bf16[512,2,256]{2,1,0:T(2,128)(2,1)S(1)} async-done(((bf16[512,2,256]{2,1,0:T(2,128)(2,1)}), bf16[512,2,256]{2,1,0:T(2,128)(2,1)S(1)}, u32[]{:S(2)}, u32[]{:S(2)}) %all-to-all-start.2) | async-done | bytes 524320 | tf_op jit(solution)/shard_map/all_to_all | solution.py:200
  443.7 5.0 fusion.135
  448.7 5.2 fusion.131
  453.9 5.0 fusion.126
  459.7 0.8 copy.60
  460.5 5.2 fusion.125
  466.5 0.8 copy.61
  467.4 13.5 %all_to_all.35 = bf16[16,32,2,256]{3,1,2,0:T(8,128)(2,1)S(1)} all-to-all(bf16[16,32,2,256]{3,1,2,0:T(8,128)(2,1)S(1)} %pad_maximum_fusion.1), channel_id=1, replica_groups=mesh['au'=16,'vert'=32] {'au'}, dimensions={0} | all-to-all | bytes 1048576 | tf_op jit(solution)/shard_map/all_to_all | solution.py:214
  480.9 1.1 copy.62
  482.0 5.4 all-to-all-start.4
  487.6 33.4 %all-to-all-done.4 = bf16[16,32,2,256]{3,0,2,1:T(8,128)(2,1)S(1)} async-done(((bf16[16,32,2,256]{3,0,2,1:T(8,128)(2,1)}), bf16[16,32,2,256]{3,0,2,1:T(8,128)(2,1)S(1)}, u32[]{:S(2)}, u32[]{:S(2)}) %all-to-all-start.4) | async-done | bytes 524320 | tf_op jit(solution)/shard_map/all_to_all | solution.py:213
  520.9 2.2 copy.63
  523.1 2.1 reshape.470
  525.2 5.0 fusion.150
  530.3 5.1 fusion.158
  535.3 5.1 fusion.156
  540.4 5.3 fusion.152
  549.7 2.1 maximum_multiply_fusion
  (267 shorter events, 51.4 us)
Async XLA Ops:
  7.2 206.9 %all-gather.2.cloned.1.call-start = ((), (), s32[]{:S(2)}) async-start(), calls=%async_computation.5 | async-start | bytes 2101248 | tf_op jit(solution)/shard_map/all_gather | solution.py:158
  10.6 329.5 %all-to-all-start = ((s32[32,2,2]{1,2,0:T(2,128)}), s32[32,2,2]{1,2,0:T(2,128)S(1)}, u32[]{:S(2)}, u32[]{:S(2)}) async-start(s32[32,2,2]{1,2,0:T(2,128)} %copy.49), calls=%async_computation | async-start | bytes 65536 | tf_op jit(solution)/shard_map/all_to_all | solution.py:189
  340.1 29.5 %all-to-all-start.1 = ((bf16[32,2,2048]{2,1,0:T(2,128)(2,1)}), bf16[32,2,2048]{2,1,0:T(2,128)(2,1)S(1)}, u32[]{:S(2)}, u32[]{:S(2)}) async-start(bf16[32,2,2048]{2,1,0:T(2,128)(2,1)} %reshape.466), calls=%async_computation.1 | async-start | bytes 524288 | tf_op jit(solution)/shard_map/all_to_all | solution.py:188
  391.0 8.0 %collective-permute-start = (bf16[32,512]{1,0:T(8,128)(2,1)S(1)}, bf16[32,512]{1,0:T(8,128)(2,1)S(1)}, u32[]{:S(2)}, u32[]{:S(2)}) collective-permute-start(bf16[32,512]{1,0:T(8,128)(2,1)S(1)} %slice.226), channel_id=1, source_target_pairs={{0,32},{32,64},{64,96},{96,128},{128,160},{160,192},{192,224},{224... | collective-permute-start | bytes 98312 | tf_op jit(solution)/shard_map/ppermute | solution.py:16
  401.5 40.5 %copy-start = (f32[512,2,256]{2,1,0:T(2,128)}, f32[512,2,256]{2,1,0:T(2,128)S(1)}, u32[]{:S(2)}) copy-start(f32[512,2,256]{2,1,0:T(2,128)S(1)} %reshape.468) | copy-start | bytes 3145732
  402.7 38.9 %all-to-all-start.2 = ((bf16[512,2,256]{2,1,0:T(2,128)(2,1)}), bf16[512,2,256]{2,1,0:T(2,128)(2,1)S(1)}, u32[]{:S(2)}, u32[]{:S(2)}) async-start(bf16[512,2,256]{2,1,0:T(2,128)(2,1)} %convert_element_type.204), calls=%async_computation.2 | async-start | bytes 1048576 | tf_op jit(solution)/shard_map/all_to_all | solution.py:200
  482.0 39.0 %all-to-all-start.4 = ((bf16[16,32,2,256]{3,0,2,1:T(8,128)(2,1)}), bf16[16,32,2,256]{3,0,2,1:T(8,128)(2,1)S(1)}, u32[]{:S(2)}, u32[]{:S(2)}) async-start(bf16[16,32,2,256]{3,0,2,1:T(8,128)(2,1)} %copy.62), calls=%async_computation.4 | async-start | bytes 1048576 | tf_op jit(solution)/shard_map/all_to_all | solution.py:213
Sparse Core Ops, SparseCore 0:
  12.6 201.5 all-gather.1
where the time goes:
time: 568 us; the launch traced here: 559 us
  waiting for transfers between devices  278 us (49%)
  other arithmetic  92.1 us (16%)
  matrix products  74.3 us (13%)
  local copies, waits for them, and re-layouts  46.4 us (8%)
  starting transfers between devices  38.5 us (7%)
  between operations  14.9 us (3%)
  blocking collectives  13.5 us (2%)
    all_gather x1, waiting for transfers between devices, on_device(): beam_table = lax.all_gather(beam_terms, ('au', 'vert'), axis=0, tiled=True)  185 us
    convert_element_type x6, other arithmetic, grid_subgrids(): weighted_re = (vis_re * cos_u - vis_im * sin_u).astype(jnp.bfloat16)  47.8 us
    all_to_all x1, waiting for transfers between devices, on_device(): lax.all_to_all(lax.all_to_all(spectra.astype(jnp.bfloat16), 'au', split_a...  33.4 us
    all_to_all x1, waiting for transfers between devices, on_device(): lax.all_to_all(uv_tile.astype(jnp.bfloat16), 'vert', split_axis=0, concat...  33 us
    all_to_all x1, waiting for transfers between devices, on_device(): lax.all_to_all(uv_send, 'vert', split_axis=0, concat_axis=0, tiled=True)  21.8 us
    neg x6, other arithmetic, grid_subgrids(): -phasor_im  21.6 us
    unnamed x4, matrix products  20.4 us
    all_to_all x1, starting transfers between devices, on_device(): lax.all_to_all(offset_send, 'vert', split_axis=0, concat_axis=0, tiled=True)  16.7 us
  transfers between devices with their start and end apart: 6, of which 5 were waited for; matrix products, arithmetic and copies ran while one was open for 23% of the time, Pallas kernels for 0%

commit v1 on v0

--- a/solution.py
+++ b/solution.py
@@ -155,7 +155,12 @@
     own_count = visibilities.shape[0]
     capacity = max(2, (2 * own_count + vertical_count - 1) // vertical_count)
     slot_count = vertical_count * capacity
-    beam_table = lax.all_gather(beam_terms, ("au", "vert"), axis=0, tiled=True)
+    beam_table = jnp.concatenate(
+        lax.all_to_all(
+            jnp.stack([beam_terms] * lax.axis_size(("au", "vert"))), ("au", "vert"), 0, 0
+        ),
+        axis=0,
+    )
     target = corners[:, 1] // tile_cols
     row_offset = corners[:, 0] - lax.axis_index("au") * tile_rows
     col_offset = corners[:, 1] - target * tile_cols

time: 568 us -> 476 us (0.84)
  waiting for transfers between devices: 278 us -> 192 us
  starting transfers between devices: 38.5 us -> 57 us
  between operations: 14.9 us -> 1.31 us
    all_gather x1 -> x0, waiting for transfers between devices: 185 us -> none  [on_device(): beam_table = lax.all_gather(beam_terms, ('au', 'vert'), axis=0, tiled=True)]
    all_to_all x0 -> x1, waiting for transfers between devices: none -> 99.4 us  [on_device(): lax.all_to_all(jnp.stack([beam_terms] * lax.axis_size(('au', 'vert'))), (...]
    all_to_all x0 -> x1, starting transfers between devices: none -> 24.3 us  [on_device(): lax.all_to_all(jnp.stack([beam_terms] * lax.axis_size(('au', 'vert'))), (...]
    all_to_all x1, starting transfers between devices: 16.7 us -> 6.21 us  [on_device(): lax.all_to_all(offset_send, 'vert', split_axis=0, concat_axis=0, tiled=True)]
  transfers between devices with their start and end apart: 6 -> 6, of which waited for: 5 -> 5; matrix products, arithmetic and copies ran while one was open for 23% -> 26% of each run, Pallas kernels for 0% -> 0%
where the time goes in v1:
time: 476 us; the launch traced here: 471 us
  waiting for transfers between devices  192 us (40%)
  other arithmetic  90 us (19%)
  matrix products  74.5 us (16%)
  starting transfers between devices  57 us (12%)
  local copies, waits for them, and re-layouts  41.8 us (9%)
  blocking collectives  13.2 us (3%)
    all_to_all x1, waiting for transfers between devices, on_device(): lax.all_to_all(jnp.stack([beam_terms] * lax.axis_size(('au', 'vert'))), (...  99.4 us
    convert_element_type x6, other arithmetic, grid_subgrids(): weighted_re = (vis_re * cos_u - vis_im * sin_u).astype(jnp.bfloat16)  47.8 us
    all_to_all x1, waiting for transfers between devices, on_device(): lax.all_to_all(lax.all_to_all(spectra.astype(jnp.bfloat16), 'au', split_a...  33.4 us
    all_to_all x1, waiting for transfers between devices, on_device(): lax.all_to_all(uv_tile.astype(jnp.bfloat16), 'vert', split_axis=0, concat...  33.2 us
    all_to_all x1, starting transfers between devices, on_device(): lax.all_to_all(jnp.stack([beam_terms] * lax.axis_size(('au', 'vert'))), (...  24.3 us
    all_to_all x1, waiting for transfers between devices, on_device(): lax.all_to_all(uv_send, 'vert', split_axis=0, concat_axis=0, tiled=True)  21.8 us
    neg x6, other arithmetic, grid_subgrids(): -phasor_im  21.6 us
    unnamed x4, matrix products  20.4 us
  transfers between devices with their start and end apart: 6, of which 5 were waited for; matrix products, arithmetic and copies ran while one was open for 26% of the time, Pallas kernels for 0%

profile of v1, /device:TPU:1, one launch (start us, length us, event | category | flops | bytes accessed | tf_op | source)
XLA Modules:
  0.0 470.9 jit_solution(4168018297234436505)
XLA Ops:
  0.6 3.1 stack.44
  3.7 24.3 %all-to-all-start.1 = ((bf16[512,1,2,1024]{3,2,1,0:T(2,128)(2,1)}), bf16[512,1,2,1024]{3,2,1,0:T(2,128)(2,1)S(1)}, u32[]{:S(2)}, u32[]{:S(2)}) async-start(bf16[512,1,2,1024]{3,2,1,0:T(2,128)(2,1)} %stack.44), calls=%async_computation.1 | async-start | bytes 4194304 | tf_op jit(solution)/shard_map/all_to_all | solution.py:159
  29.4 99.4 %all-to-all-done.1 = bf16[512,1,2,1024]{3,2,1,0:T(2,128)(2,1)S(1)} async-done(((bf16[512,1,2,1024]{3,2,1,0:T(2,128)(2,1)}), bf16[512,1,2,1024]{3,2,1,0:T(2,128)(2,1)S(1)}, u32[]{:S(2)}, u32[]{:S(2)}) %all-to-all-start.1) | async-done | bytes 2097184 | tf_op jit(solution)/shard_map/all_to_all | solution.py:159
  128.9 6.2 %all-to-all-start = ((s32[32,2,2]{1,2,0:T(2,128)}), s32[32,2,2]{1,2,0:T(2,128)S(1)}, u32[]{:S(2)}, u32[]{:S(2)}) async-start(s32[32,2,2]{1,2,0:T(2,128)} %copy.49), calls=%async_computation | async-start | bytes 65536 | tf_op jit(solution)/shard_map/all_to_all | solution.py:194
  135.1 0.8 gather_fusion
  135.8 0.8 gather_fusion.1
  136.9 116.0 %while.15 = (s32[]{:T(128)}, bf16[6,4,2048]{2,1,0:T(4,128)(2,1)S(1)}, bf16[6,4,2,2048]{3,2,1,0:T(2,128)(2,1)}, f32[6,4,2,128]{3,2,1,0:T(2,128)}, f32[16]{0:T(128...) while((s32[]{:T(128)}, ...), condition=%wide.region_2.4_spmd, body=%wide.region_1.3_spmd.sunk | while | flops 94977376 | bytes 7133457 | solution.py:119
  136.9 0.7 constant_dynamic-slice_fusion.9
  138.3 0.8 constant_dynamic-slice_fusion.8
  139.2 8.0 %fusion.347 = (bf16[4,32,2048]{2,1,0:T(8,128)(2,1)S(1)}, bf16[4,32,2048]{2,1,0:T(8,128)(2,1)S(1)}, bf16[4,32,2048]{2,1,0:T(8,128)(2,1)S(1)}, bf16[4,32,2048]{2,1,0:T(8,128)(2,1)S(1)}) fusion(f32[4,2048]{1,0:T(4,128)S(1)} %get-tuple-element.319, f32[4,2048]{1,0:T(4,128)S(1)} %get-tuple-element.322, f32[32]{0:T(128)S(1)} %fusion.346, ...), kind=kLoop, calls=%fused_computation.30.clone.1 | loop fusion | flops 3145728 | bytes 2228352 | tf_op jit(solution)/shard_map/while/body/eval_jaxpr/convert_element_type | solution.py:71
  147.1 3.6 fusion.348
  150.7 0.8 fusion.349
  156.2 0.7 constant_dynamic-slice_fusion.9
  157.6 0.8 constant_dynamic-slice_fusion.8
  158.5 8.0 %fusion.347 = (bf16[4,32,2048]{2,1,0:T(8,128)(2,1)S(1)}, bf16[4,32,2048]{2,1,0:T(8,128)(2,1)S(1)}, bf16[4,32,2048]{2,1,0:T(8,128)(2,1)S(1)}, bf16[4,32,2048]{2,1,0:T(8,128)(2,1)S(1)}) fusion(f32[4,2048]{1,0:T(4,128)S(1)} %get-tuple-element.319, f32[4,2048]{1,0:T(4,128)S(1)} %get-tuple-element.322, f32[32]{0:T(128)S(1)} %fusion.346, ...), kind=kLoop, calls=%fused_computation.30.clone.1 | loop fusion | flops 3145728 | bytes 2228352 | tf_op jit(solution)/shard_map/while/body/eval_jaxpr/convert_element_type | solution.py:71
  166.5 3.6 fusion.348
  170.1 0.8 fusion.349
  177.0 0.8 constant_dynamic-slice_fusion.8
  177.8 8.0 %fusion.347 = (bf16[4,32,2048]{2,1,0:T(8,128)(2,1)S(1)}, bf16[4,32,2048]{2,1,0:T(8,128)(2,1)S(1)}, bf16[4,32,2048]{2,1,0:T(8,128)(2,1)S(1)}, bf16[4,32,2048]{2,1,0:T(8,128)(2,1)S(1)}) fusion(f32[4,2048]{1,0:T(4,128)S(1)} %get-tuple-element.319, f32[4,2048]{1,0:T(4,128)S(1)} %get-tuple-element.322, f32[32]{0:T(128)S(1)} %fusion.346, ...), kind=kLoop, calls=%fused_computation.30.clone.1 | loop fusion | flops 3145728 | bytes 2228352 | tf_op jit(solution)/shard_map/while/body/eval_jaxpr/convert_element_type | solution.py:71
  185.8 3.6 fusion.348
  189.4 0.8 fusion.349
  196.3 0.8 constant_dynamic-slice_fusion.8
  197.2 8.0 %fusion.347 = (bf16[4,32,2048]{2,1,0:T(8,128)(2,1)S(1)}, bf16[4,32,2048]{2,1,0:T(8,128)(2,1)S(1)}, bf16[4,32,2048]{2,1,0:T(8,128)(2,1)S(1)}, bf16[4,32,2048]{2,1,0:T(8,128)(2,1)S(1)}) fusion(f32[4,2048]{1,0:T(4,128)S(1)} %get-tuple-element.319, f32[4,2048]{1,0:T(4,128)S(1)} %get-tuple-element.322, f32[32]{0:T(128)S(1)} %fusion.346, ...), kind=kLoop, calls=%fused_computation.30.clone.1 | loop fusion | flops 3145728 | bytes 2228352 | tf_op jit(solution)/shard_map/while/body/eval_jaxpr/convert_element_type | solution.py:71
  205.1 3.6 fusion.348
  208.7 0.8 fusion.349
  215.6 0.8 constant_dynamic-slice_fusion.8
  216.5 8.0 %fusion.347 = (bf16[4,32,2048]{2,1,0:T(8,128)(2,1)S(1)}, bf16[4,32,2048]{2,1,0:T(8,128)(2,1)S(1)}, bf16[4,32,2048]{2,1,0:T(8,128)(2,1)S(1)}, bf16[4,32,2048]{2,1,0:T(8,128)(2,1)S(1)}) fusion(f32[4,2048]{1,0:T(4,128)S(1)} %get-tuple-element.319, f32[4,2048]{1,0:T(4,128)S(1)} %get-tuple-element.322, f32[32]{0:T(128)S(1)} %fusion.346, ...), kind=kLoop, calls=%fused_computation.30.clone.1 | loop fusion | flops 3145728 | bytes 2228352 | tf_op jit(solution)/shard_map/while/body/eval_jaxpr/convert_element_type | solution.py:71
  224.5 3.6 fusion.348
  228.1 0.8 fusion.349
  235.0 0.8 constant_dynamic-slice_fusion.8
  235.8 8.0 %fusion.347 = (bf16[4,32,2048]{2,1,0:T(8,128)(2,1)S(1)}, bf16[4,32,2048]{2,1,0:T(8,128)(2,1)S(1)}, bf16[4,32,2048]{2,1,0:T(8,128)(2,1)S(1)}, bf16[4,32,2048]{2,1,0:T(8,128)(2,1)S(1)}) fusion(f32[4,2048]{1,0:T(4,128)S(1)} %get-tuple-element.319, f32[4,2048]{1,0:T(4,128)S(1)} %get-tuple-element.322, f32[32]{0:T(128)S(1)} %fusion.346, ...), kind=kLoop, calls=%fused_computation.30.clone.1 | loop fusion | flops 3145728 | bytes 2228352 | tf_op jit(solution)/shard_map/while/body/eval_jaxpr/convert_element_type | solution.py:71
  243.8 3.6 fusion.348
  247.4 0.8 fusion.349
  253.1 0.9 reshape.473
  254.0 12.6 %all-to-all-start.2 = ((bf16[32,2,2048]{2,1,0:T(2,128)(2,1)}), bf16[32,2,2048]{2,1,0:T(2,128)(2,1)S(1)}, u32[]{:S(2)}, u32[]{:S(2)}) async-start(bf16[32,2,2048]{2,1,0:T(2,128)(2,1)} %reshape.473), calls=%async_computation.2 | async-start | bytes 524288 | tf_op jit(solution)/shard_map/all_to_all | solution.py:193
  267.0 21.8 %all-to-all-done.2 = bf16[32,2,2048]{2,1,0:T(2,128)(2,1)S(1)} async-done(((bf16[32,2,2048]{2,1,0:T(2,128)(2,1)}), bf16[32,2,2048]{2,1,0:T(2,128)(2,1)S(1)}, u32[]{:S(2)}, u32[]{:S(2)}) %all-to-all-start.2) | async-done | bytes 262176 | tf_op jit(solution)/shard_map/all_to_all | solution.py:193
  289.2 1.0 convolution_bitcast_fusion
  290.3 3.9 copy.56
  294.2 2.4 copy.81
  296.6 13.5 %scatter_custom_fusion = f32[544,512]{1,0:T(8,128)S(1)} fusion(s32[2048]{0:T(1024)S(1)} %reshape.500, f32[2048,512]{1,0:T(8,128)} %bitcast.256, f32[]{:T(128)} %constant.250.clone.1), kind=kCustom, calls=%fused_computation.192 | custom fusion | flops 1048576 | bytes 1114624 | tf_op jit(solution)/shard_map/scatter-add | solution.py:142
  310.1 2.9 collective-permute-start
  313.0 1.0 slice.178
  314.0 4.0 collective-permute-done
  318.7 1.9 reshape.475
  320.6 1.2 convert_element_type.204
  321.8 5.6 %all-to-all-start.3 = ((bf16[512,2,256]{2,1,0:T(2,128)(2,1)}), bf16[512,2,256]{2,1,0:T(2,128)(2,1)S(1)}, u32[]{:S(2)}, u32[]{:S(2)}) async-start(bf16[512,2,256]{2,1,0:T(2,128)(2,1)} %convert_element_type.204), calls=%async_computation.3 | async-start | bytes 1048576 | tf_op jit(solution)/shard_map/all_to_all | solution.py:205
  327.5 33.2 %all-to-all-done.3 = bf16[512,2,256]{2,1,0:T(2,128)(2,1)S(1)} async-done(((bf16[512,2,256]{2,1,0:T(2,128)(2,1)}), bf16[512,2,256]{2,1,0:T(2,128)(2,1)S(1)}, u32[]{:S(2)}, u32[]{:S(2)}) %all-to-all-start.3) | async-done | bytes 524320 | tf_op jit(solution)/shard_map/all_to_all | solution.py:205
  362.8 5.0 %fusion.135 = f32[512,16,16]{0,2,1:T(8,128)S(1)} fusion(f32[16,16,512]{2,0,1:T(8,128)S(1)} %convolution_add_fusion.3, f32[16,16,512]{2,0,1:T(8,128)S(1)} %convolution_subtract_fusion.3, f32[16,512]{1,0:T(8,128)S(1)} %get-tuple-element.249, f32[16,512]{1,0:T(8,128)S(1)} %get-tuple-element.250), kind=kOutput, calls=%fused_computation.186 | convolution fusion | flops 809369600 | bytes 1638400 | tf_op jit(solution)/shard_map/ukj,pj->pku/dot_general | solution.py:22
  367.8 5.5 %fusion.131 = f32[512,16,16]{0,2,1:T(8,128)S(1)} fusion(f32[16,16,512]{2,0,1:T(8,128)S(1)} %convolution_add_fusion.3, f32[16,16,512]{2,0,1:T(8,128)S(1)} %convolution_subtract_fusion.3, f32[16,512]{1,0:T(8,128)S(1)} %get-tuple-element.249, f32[16,512]{1,0:T(8,128)S(1)} %get-tuple-element.250), kind=kOutput, calls=%fused_computation.182 | convolution fusion | flops 809369600 | bytes 1638400 | tf_op jit(solution)/shard_map/ukj,pj->pku/dot_general | solution.py:25
  373.3 5.0 %fusion.126 = bf16[512,16,16]{0,1,2:T(8,128)(2,1)S(1)} fusion(f32[512,16,16]{0,2,1:T(8,128)S(1)} %fusion.135, f32[16,16,512]{2,0,1:T(8,128)S(1)} %convolution_add_fusion.3, f32[16,16,512]{2,0,1:T(8,128)S(1)} %convolution_subtract_fusion.3, f32[16,512]{1,0:T(8,128)S(1)} %get-tuple-element.249, f32[16,512]{1,0:T(8,128)S(1)} %get-tuple-element.250), kind=kOutput, calls=%fused_computation.175 | convolution fusion | flops 809631744 | bytes 1900544 | tf_op jit(solution)/shard_map/ukj,pj->pku/dot_general | solution.py:22
  379.0 0.8 copy.60
  379.9 5.2 %fusion.125 = bf16[512,16,16]{0,1,2:T(8,128)(2,1)S(1)} fusion(f32[512,16,16]{0,2,1:T(8,128)S(1)} %fusion.131, f32[16,16,512]{2,0,1:T(8,128)S(1)} %convolution_add_fusion.3, f32[16,16,512]{2,0,1:T(8,128)S(1)} %convolution_subtract_fusion.3, f32[16,512]{1,0:T(8,128)S(1)} %get-tuple-element.249, f32[16,512]{1,0:T(8,128)S(1)} %get-tuple-element.250), kind=kOutput, calls=%fused_computation.174 | convolution fusion | flops 809631744 | bytes 1900544 | tf_op jit(solution)/shard_map/ukj,pj->pku/dot_general | solution.py:25
  385.8 0.8 copy.61
  386.7 13.2 %all_to_all.40 = bf16[16,32,2,256]{3,1,2,0:T(8,128)(2,1)S(1)} all-to-all(bf16[16,32,2,256]{3,1,2,0:T(8,128)(2,1)S(1)} %pad_maximum_fusion.1), channel_id=1, replica_groups=mesh['au'=16,'vert'=32] {'au'}, dimensions={0} | all-to-all | bytes 1048576 | tf_op jit(solution)/shard_map/all_to_all | solution.py:219
  399.9 1.1 copy.62
  401.0 5.4 %all-to-all-start.5 = ((bf16[16,32,2,256]{3,0,2,1:T(8,128)(2,1)}), bf16[16,32,2,256]{3,0,2,1:T(8,128)(2,1)S(1)}, u32[]{:S(2)}, u32[]{:S(2)}) async-start(bf16[16,32,2,256]{3,0,2,1:T(8,128)(2,1)} %copy.62), calls=%async_computation.5 | async-start | bytes 1048576 | tf_op jit(solution)/shard_map/all_to_all | solution.py:218
  406.6 33.4 %all-to-all-done.5 = bf16[16,32,2,256]{3,0,2,1:T(8,128)(2,1)S(1)} async-done(((bf16[16,32,2,256]{3,0,2,1:T(8,128)(2,1)}), bf16[16,32,2,256]{3,0,2,1:T(8,128)(2,1)S(1)}, u32[]{:S(2)}, u32[]{:S(2)}) %all-to-all-start.5) | async-done | bytes 524320 | tf_op jit(solution)/shard_map/all_to_all | solution.py:218
  439.9 2.2 copy.63
  442.1 2.1 reshape.477
  444.2 5.0 %fusion.150 = f32[512,256]{0,1:S(1)} fusion(bf16[512,256]{0,1:T(8,128)(2,1)S(1)} %bitcast.271), kind=kOutput, calls=%fused_computation.206 | convolution fusion | flops 808976384 | bytes 786432
  449.3 5.1 %fusion.158 = f32[512,256]{0,1:S(1)} fusion(bf16[512,256]{0,1:T(8,128)(2,1)S(1)} %bitcast.272), kind=kOutput, calls=%fused_computation.209 | convolution fusion | flops 808976384 | bytes 786432
  454.3 5.1 %fusion.156 = f32[512,256]{0,1:S(1)} fusion(bf16[512,256]{0,1:T(8,128)(2,1)S(1)} %bitcast.269), kind=kOutput, calls=%fused_computation.208 | convolution fusion | flops 808976384 | bytes 786432
  459.4 5.2 %fusion.152 = f32[512,256]{0,1:S(1)} fusion(bf16[512,256]{0,1:T(8,128)(2,1)S(1)} %bitcast.270), kind=kOutput, calls=%fused_computation.207 | convolution fusion | flops 808976384 | bytes 786432
  468.7 2.1 maximum_multiply_fusion
  (275 shorter events, 45.5 us)
Async XLA Ops:
  3.7 24.3 %copy-start.4 = (f32[24]{0:T(128)S(1)}, f32[24]{0:T(128)}, u32[]{:S(2)}) copy-start(f32[24]{0:T(128)} %param.16) | copy-start | bytes 292
  3.7 24.4 %copy-start.2 = (s32[24,2]{0,1:T(2,128)S(1)}, s32[24,2]{0,1:T(2,128)}, u32[]{:S(2)}) copy-start(s32[24,2]{0,1:T(2,128)} %param.18) | copy-start | bytes 580
  3.7 25.7 %copy-start.3 = (s32[24,2]{0,1:T(2,128)S(1)}, s32[24,2]{0,1:T(2,128)}, u32[]{:S(2)}) copy-start(s32[24,2]{0,1:T(2,128)} %param.17) | copy-start | bytes 580
  3.7 133.1 %copy-start.1 = (f32[16]{0:T(128)S(1)}, f32[16]{0:T(128)}, u32[]{:S(2)}) copy-start(f32[16]{0:T(128)} %param.15) | copy-start | bytes 196
  3.7 125.1 %all-to-all-start.1 = ((bf16[512,1,2,1024]{3,2,1,0:T(2,128)(2,1)}), bf16[512,1,2,1024]{3,2,1,0:T(2,128)(2,1)S(1)}, u32[]{:S(2)}, u32[]{:S(2)}) async-start(bf16[512,1,2,1024]{3,2,1,0:T(2,128)(2,1)} %stack.44), calls=%async_computation.1 | async-start | bytes 4194304 | tf_op jit(solution)/shard_map/all_to_all | solution.py:159
  128.9 125.2 %all-to-all-start = ((s32[32,2,2]{1,2,0:T(2,128)}), s32[32,2,2]{1,2,0:T(2,128)S(1)}, u32[]{:S(2)}, u32[]{:S(2)}) async-start(s32[32,2,2]{1,2,0:T(2,128)} %copy.49), calls=%async_computation | async-start | bytes 65536 | tf_op jit(solution)/shard_map/all_to_all | solution.py:194
  254.0 34.7 %all-to-all-start.2 = ((bf16[32,2,2048]{2,1,0:T(2,128)(2,1)}), bf16[32,2,2048]{2,1,0:T(2,128)(2,1)S(1)}, u32[]{:S(2)}, u32[]{:S(2)}) async-start(bf16[32,2,2048]{2,1,0:T(2,128)(2,1)} %reshape.473), calls=%async_computation.2 | async-start | bytes 524288 | tf_op jit(solution)/shard_map/all_to_all | solution.py:193
  310.1 8.0 %collective-permute-start = (bf16[32,512]{1,0:T(8,128)(2,1)S(1)}, bf16[32,512]{1,0:T(8,128)(2,1)S(1)}, u32[]{:S(2)}, u32[]{:S(2)}) collective-permute-start(bf16[32,512]{1,0:T(8,128)(2,1)S(1)} %slice.226), channel_id=1, source_target_pairs={{0,32},{32,64},{64,96},{96,128},{128,160},{160,192},{192,224},{224... | collective-permute-start | bytes 98312 | tf_op jit(solution)/shard_map/ppermute | solution.py:16
  320.6 40.5 %copy-start = (f32[512,2,256]{2,1,0:T(2,128)}, f32[512,2,256]{2,1,0:T(2,128)S(1)}, u32[]{:S(2)}) copy-start(f32[512,2,256]{2,1,0:T(2,128)S(1)} %reshape.475) | copy-start | bytes 3145732
  321.8 38.9 %all-to-all-start.3 = ((bf16[512,2,256]{2,1,0:T(2,128)(2,1)}), bf16[512,2,256]{2,1,0:T(2,128)(2,1)S(1)}, u32[]{:S(2)}, u32[]{:S(2)}) async-start(bf16[512,2,256]{2,1,0:T(2,128)(2,1)} %convert_element_type.204), calls=%async_computation.3 | async-start | bytes 1048576 | tf_op jit(solution)/shard_map/all_to_all | solution.py:205
  401.0 39.0 %all-to-all-start.5 = ((bf16[16,32,2,256]{3,0,2,1:T(8,128)(2,1)}), bf16[16,32,2,256]{3,0,2,1:T(8,128)(2,1)S(1)}, u32[]{:S(2)}, u32[]{:S(2)}) async-start(bf16[16,32,2,256]{3,0,2,1:T(8,128)(2,1)} %copy.62), calls=%async_computation.5 | async-start | bytes 1048576 | tf_op jit(solution)/shard_map/all_to_all | solution.py:218
